TPU v7x, 32 devices: a whole 2x2x4 slice. The times are simulated.
32 devices in a mesh: dp: 8 (over z, x), shard: 4 (over y, core).
Axes of the slice: x: 2, y: 2, z: 4, core: 2. Of those that a mesh axis runs over, the one named last changes fastest.
Arguments:
- tokens: bfloat16 [8192, 2048], P('dp'), may hold values from -6 to 6
- block_ids: int32 [8, 1024], P('dp'), may hold values from 0 to 7, never falling along the last dimension, each value on 1 to 256 neighbouring positions
- cotangent: bfloat16 [8192, 2048], P('dp'), may hold values from -12 to 12
- gain_first: float32 [2048], P('dp'), may hold values from 0.3 to 2.5
- w_query: float32 [2048, 2048], P('dp', 'shard'), may hold values from -0.125 to 0.125
- w_key: float32 [2048, 512], P('dp', 'shard'), may hold values from -0.125 to 0.125
- w_value: float32 [2048, 512], P('dp', 'shard'), may hold values from -0.125 to 0.125
- w_output: float32 [2048, 2048], P('shard', 'dp'), may hold values from -2 to 2
- gain_second: float32 [2048], P('dp'), may hold values from 0.3 to 2.5
- w_gate: float32 [2048, 8192], P('dp', 'shard'), may hold values from -0.125 to 0.125
- w_up: float32 [2048, 8192], P('dp', 'shard'), may hold values from -0.125 to 0.125
- w_down: float32 [8192, 2048], P('shard', 'dp'), may hold values from -0.0625 to 0.0625
- moment_first: float32 [2048], P('dp'), may hold values from -6 to 6
- moment_query: float32 [2048, 2048], P('dp', 'shard'), may hold values from -4 to 4
- moment_key: float32 [2048, 512], P('dp', 'shard'), may hold values from -4 to 4
- moment_value: float32 [2048, 512], P('dp', 'shard'), may hold values from -4 to 4
- moment_output: float32 [2048, 2048], P('shard', 'dp'), may hold values from -4 to 4
- moment_second: float32 [2048], P('dp'), may hold values from -6 to 6
- moment_gate: float32 [2048, 8192], P('dp', 'shard'), may hold values from -4 to 4
- moment_up: float32 [2048, 8192], P('dp', 'shard'), may hold values from -4 to 4
- moment_down: float32 [8192, 2048], P('shard', 'dp'), may hold values from -4 to 4
- step: int32 [], replicated, may hold values from 1000 to 1999
- rate: float32 [], replicated, may hold values from 0.6 to 1.2
Outputs:
- output: bfloat16 [8192, 2048], P('dp')
- input_grad: float32 [8192, 2048], P('dp')
- global_norm: float32 [], replicated
- momentum_first: float32 [2048], P('dp')
- momentum_query: float32 [2048, 2048], P('dp', 'shard')
- momentum_key: float32 [2048, 512], P('dp', 'shard')
- momentum_value: float32 [2048, 512], P('dp', 'shard')
- momentum_output: float32 [2048, 2048], P('shard', 'dp')
- momentum_second: float32 [2048], P('dp')
- momentum_gate: float32 [2048, 8192], P('dp', 'shard')
- momentum_up: float32 [2048, 8192], P('dp', 'shard')
- momentum_down: float32 [8192, 2048], P('shard', 'dp')
- updated_first: float32 [2048], P('dp')
- updated_query: float32 [2048, 2048], P('dp', 'shard')
- updated_key: float32 [2048, 512], P('dp', 'shard')
- updated_value: float32 [2048, 512], P('dp', 'shard')
- updated_output: float32 [2048, 2048], P('shard', 'dp')
- updated_second: float32 [2048], P('dp')
- updated_gate: float32 [2048, 8192], P('dp', 'shard')
- updated_up: float32 [2048, 8192], P('dp', 'shard')
- updated_down: float32 [8192, 2048], P('shard', 'dp')
Inputs may be any that keep to these rules, and one draw needn't show every extreme that they name: `block_ids`: along each row the block numbers never fall, every number 0 to 7 appears, and a block holds 1 to 256 positions.
All inputs are finite; a program needn't handle non-finite values.
Results may differ from a plain program's by a relative error of at most 0.02.
Values may be sent and summed in bfloat16 or wider, within the bound.
A program may use at most 256 MiB of HBM per device.

v0:
```python
import math
import jax
import jax.numpy as jnp
from jax import lax
from jax.sharding import PartitionSpec as P

H = 32
KV = 8
HD = 64
CLIP = 4096
WARMUP = 2000
EPS = 1e-05
THETA = 10000000.0
NEGATIVE = -1e30


def inverse_rms(values):
    return lax.rsqrt(jnp.mean(values * values, axis=1, keepdims=True) + EPS)


def norm_back(values, inverse, gain, grad_normed):
    scaled = grad_normed * gain[None, :]
    gain_grad = jnp.sum(grad_normed * values * inverse, axis=0)
    grad_values = inverse * scaled - values * inverse**3 * jnp.mean(
        scaled * values, axis=1, keepdims=True
    )
    return (gain_grad, grad_values)


def angle_table(count, length):
    positions = (jnp.arange(count, dtype=jnp.int32) % length).astype(jnp.float32)
    powers = -2.0 * jnp.arange(HD // 2, dtype=jnp.float32) / HD
    angles = positions[:, None] * jnp.power(THETA, powers)[None, :]
    return (jnp.cos(angles)[:, None, :], jnp.sin(angles)[:, None, :])


def rotate(values, cosine, sine):
    half = values.shape[-1] // 2
    first = values[..., :half]
    second = values[..., half:]
    return jnp.concatenate(
        [first * cosine - second * sine, second * cosine + first * sine], axis=-1
    )


def unrotate(grads, cosine, sine):
    half = grads.shape[-1] // 2
    first = grads[..., :half]
    second = grads[..., half:]
    return jnp.concatenate(
        [first * cosine + second * sine, second * cosine - first * sine], axis=-1
    )


def to_items(values, seqs, length):
    shaped = values.reshape((seqs, length) + values.shape[1:])
    moved = jnp.moveaxis(shaped, 2, 1)
    return moved.reshape((seqs * values.shape[1], length) + values.shape[2:])


def from_items(items, seqs):
    groups = items.shape[0] // seqs
    shaped = items.reshape((seqs, groups) + items.shape[1:])
    moved = jnp.moveaxis(shaped, 1, 2)
    return moved.reshape((seqs * items.shape[1], groups) + items.shape[2:])


def item_scores(query, key, blocks, scale):
    scores = jnp.einsum("qgd,jd->gqj", query, key, preferred_element_type=jnp.float32) * scale
    allowed = blocks[None, :] <= blocks[:, None]
    return jnp.where(allowed[None], scores, NEGATIVE)


def attend_forward(scale):

    def run(parts):
        query, key, value, blocks = parts
        scores = item_scores(query, key, blocks, scale)
        peak = jnp.max(scores, axis=2, keepdims=True)
        weights = jnp.exp(scores - peak)
        total = jnp.sum(weights, axis=2, keepdims=True)
        probs = (weights / total).astype(jnp.bfloat16)
        mixed = jnp.einsum("gqj,jd->qgd", probs, value, preferred_element_type=jnp.float32)
        return (mixed.astype(jnp.bfloat16), peak, total)

    return run


def attend_backward(scale):

    def run(parts):
        query, key, value, blocks, peak, total, grad_mixed = parts
        scores = item_scores(query, key, blocks, scale)
        probs = jnp.exp(scores - peak) / total
        probs_low = probs.astype(jnp.bfloat16)
        grad_value = jnp.einsum(
            "gqj,qgd->jd", probs_low, grad_mixed, preferred_element_type=jnp.float32
        )
        grad_probs = jnp.einsum(
            "qgd,jd->gqj", grad_mixed, value, preferred_element_type=jnp.float32
        )
        grad_scores = (
            probs * (grad_probs - jnp.sum(probs * grad_probs, axis=2, keepdims=True))
        ).astype(jnp.bfloat16)
        grad_query = (
            jnp.einsum("gqj,jd->qgd", grad_scores, key, preferred_element_type=jnp.float32) * scale
        )
        grad_key = (
            jnp.einsum("gqj,qgd->jd", grad_scores, query, preferred_element_type=jnp.float32)
            * scale
        )
        return (grad_query, grad_key, grad_value)

    return run


def on_device(
    tokens,
    block_ids,
    cotangent,
    gain_first,
    w_query,
    w_key,
    w_value,
    w_output,
    gain_second,
    w_gate,
    w_up,
    w_down,
    moment_first,
    moment_query,
    moment_key,
    moment_value,
    moment_output,
    moment_second,
    moment_gate,
    moment_up,
    moment_down,
    step,
    rate,
):
    seqs, length = block_ids.shape
    count = tokens.shape[0]
    scale = 1.0 / math.sqrt(HD)
    group = H // KV
    (
        gain_one,
        query_weight,
        key_weight,
        value_weight,
        output_weight,
        gain_two,
        gate_weight,
        up_weight,
        down_weight,
    ) = (
        lax.all_gather(gain_first.astype(jnp.bfloat16), "dp", axis=0, tiled=True),
        lax.all_gather(w_query.astype(jnp.bfloat16), "dp", axis=0, tiled=True),
        lax.all_gather(w_key.astype(jnp.bfloat16), "dp", axis=0, tiled=True),
        lax.all_gather(w_value.astype(jnp.bfloat16), "dp", axis=0, tiled=True),
        lax.all_gather(w_output.astype(jnp.bfloat16), "dp", axis=1, tiled=True),
        lax.all_gather(gain_second.astype(jnp.bfloat16), "dp", axis=0, tiled=True),
        lax.all_gather(w_gate.astype(jnp.bfloat16), "dp", axis=0, tiled=True),
        lax.all_gather(w_up.astype(jnp.bfloat16), "dp", axis=0, tiled=True),
        lax.all_gather(w_down.astype(jnp.bfloat16), "dp", axis=1, tiled=True),
    )
    heads_local = query_weight.shape[1] // HD
    kv_local = key_weight.shape[1] // HD
    inputs = tokens.astype(jnp.float32)
    inverse_first = inverse_rms(inputs)
    gain_one_wide = gain_one.astype(jnp.float32)
    normed = (inputs * inverse_first * gain_one_wide[None, :]).astype(jnp.bfloat16)
    cosine, sine = angle_table(count, length)
    query = rotate(
        jnp.dot(normed, query_weight, preferred_element_type=jnp.float32).reshape(
            count, heads_local, HD
        ),
        cosine,
        sine,
    ).astype(jnp.bfloat16)
    key = rotate(
        jnp.dot(normed, key_weight, preferred_element_type=jnp.float32).reshape(
            count, kv_local, HD
        ),
        cosine,
        sine,
    ).astype(jnp.bfloat16)
    value = (
        jnp.dot(normed, value_weight, preferred_element_type=jnp.float32)
        .astype(jnp.bfloat16)
        .reshape(count, kv_local, HD)
    )
    query_items = to_items(query.reshape(count, kv_local, group, HD), seqs, length)
    key_items = to_items(key, seqs, length)
    value_items = to_items(value, seqs, length)
    block_items = jnp.repeat(block_ids, kv_local, axis=0)
    mixed_items, peak, total = lax.map(
        attend_forward(scale), (query_items, key_items, value_items, block_items)
    )
    mixed = from_items(mixed_items, seqs).reshape(count, heads_local * HD)
    hidden = inputs + lax.psum(
        jnp.dot(mixed, output_weight, preferred_element_type=jnp.float32).astype(jnp.bfloat16),
        "shard",
    ).astype(jnp.float32)
    inverse_second = inverse_rms(hidden)
    gain_two_wide = gain_two.astype(jnp.float32)
    normed_two = (hidden * inverse_second * gain_two_wide[None, :]).astype(jnp.bfloat16)
    gate = jnp.dot(normed_two, gate_weight, preferred_element_type=jnp.float32)
    up = jnp.dot(normed_two, up_weight, preferred_element_type=jnp.float32)
    sigmoid_gate = jax.nn.sigmoid(gate)
    activated = (gate * sigmoid_gate * up).astype(jnp.bfloat16)
    result = hidden + lax.psum(
        jnp.dot(activated, down_weight, preferred_element_type=jnp.float32).astype(jnp.bfloat16),
        "shard",
    ).astype(jnp.float32)
    output = result.astype(jnp.bfloat16)
    grad_result = cotangent.astype(jnp.float32)
    grad_down_weight = jnp.einsum(
        "tf,td->fd", activated, cotangent, preferred_element_type=jnp.float32
    )
    grad_act = jnp.einsum("td,fd->tf", cotangent, down_weight, preferred_element_type=jnp.float32)
    grad_gate_in = (grad_act * up * sigmoid_gate * (1.0 + gate * (1.0 - sigmoid_gate))).astype(
        jnp.bfloat16
    )
    grad_up_in = (grad_act * gate * sigmoid_gate).astype(jnp.bfloat16)
    grad_gate_weight = jnp.einsum(
        "tc,tf->cf", normed_two, grad_gate_in, preferred_element_type=jnp.float32
    )
    grad_up_weight = jnp.einsum(
        "tc,tf->cf", normed_two, grad_up_in, preferred_element_type=jnp.float32
    )
    partial_two = jnp.einsum(
        "tf,cf->tc", grad_gate_in, gate_weight, preferred_element_type=jnp.float32
    ) + jnp.einsum("tf,cf->tc", grad_up_in, up_weight, preferred_element_type=jnp.float32)
    grad_normed_two = lax.psum(partial_two.astype(jnp.bfloat16), "shard").astype(jnp.float32)
    gain_grad_two, grad_through = norm_back(hidden, inverse_second, gain_two_wide, grad_normed_two)
    grad_hidden = grad_result + grad_through
    grad_hidden_low = grad_hidden.astype(jnp.bfloat16)
    grad_output_weight = jnp.einsum(
        "tk,td->kd", mixed, grad_hidden_low, preferred_element_type=jnp.float32
    )
    grad_mixed = jnp.einsum(
        "td,kd->tk", grad_hidden_low, output_weight, preferred_element_type=jnp.float32
    ).astype(jnp.bfloat16)
    grad_mixed_items = to_items(grad_mixed.reshape(count, kv_local, group, HD), seqs, length)
    grad_query_items, grad_key_items, grad_value_items = lax.map(
        attend_backward(scale),
        (query_items, key_items, value_items, block_items, peak, total, grad_mixed_items),
    )
    grad_query_in = (
        unrotate(from_items(grad_query_items, seqs).reshape(count, heads_local, HD), cosine, sine)
        .astype(jnp.bfloat16)
        .reshape(count, heads_local * HD)
    )
    grad_key_in = (
        unrotate(from_items(grad_key_items, seqs), cosine, sine)
        .astype(jnp.bfloat16)
        .reshape(count, kv_local * HD)
    )
    grad_value_in = (
        from_items(grad_value_items, seqs).astype(jnp.bfloat16).reshape(count, kv_local * HD)
    )
    grad_query_weight = jnp.einsum(
        "tc,tk->ck", normed, grad_query_in, preferred_element_type=jnp.float32
    )
    grad_key_weight = jnp.einsum(
        "tc,tk->ck", normed, grad_key_in, preferred_element_type=jnp.float32
    )
    grad_value_weight = jnp.einsum(
        "tc,tk->ck", normed, grad_value_in, preferred_element_type=jnp.float32
    )
    partial_one = jnp.einsum(
        "tk,ck->tc", grad_query_in, query_weight, preferred_element_type=jnp.float32
    )
    partial_one = partial_one + jnp.einsum(
        "tk,ck->tc", grad_key_in, key_weight, preferred_element_type=jnp.float32
    )
    partial_one = partial_one + jnp.einsum(
        "tk,ck->tc", grad_value_in, value_weight, preferred_element_type=jnp.float32
    )
    grad_normed = lax.psum(partial_one.astype(jnp.bfloat16), "shard").astype(jnp.float32)
    gain_grad_one, grad_inner = norm_back(inputs, inverse_first, gain_one_wide, grad_normed)
    input_grad = grad_hidden + grad_inner
    owned = (
        lax.psum_scatter(
            gain_grad_one.astype(jnp.bfloat16), "dp", scatter_dimension=0, tiled=True
        ).astype(jnp.float32),
        lax.psum_scatter(
            grad_query_weight.astype(jnp.bfloat16), "dp", scatter_dimension=0, tiled=True
        ).astype(jnp.float32),
        lax.psum_scatter(
            grad_key_weight.astype(jnp.bfloat16), "dp", scatter_dimension=0, tiled=True
        ).astype(jnp.float32),
        lax.psum_scatter(
            grad_value_weight.astype(jnp.bfloat16), "dp", scatter_dimension=0, tiled=True
        ).astype(jnp.float32),
        lax.psum_scatter(
            grad_output_weight.astype(jnp.bfloat16), "dp", scatter_dimension=1, tiled=True
        ).astype(jnp.float32),
        lax.psum_scatter(
            gain_grad_two.astype(jnp.bfloat16), "dp", scatter_dimension=0, tiled=True
        ).astype(jnp.float32),
        lax.psum_scatter(
            grad_gate_weight.astype(jnp.bfloat16), "dp", scatter_dimension=0, tiled=True
        ).astype(jnp.float32),
        lax.psum_scatter(
            grad_up_weight.astype(jnp.bfloat16), "dp", scatter_dimension=0, tiled=True
        ).astype(jnp.float32),
        lax.psum_scatter(
            grad_down_weight.astype(jnp.bfloat16), "dp", scatter_dimension=1, tiled=True
        ).astype(jnp.float32),
    )
    first_shard = (lax.axis_index("shard") == 0).astype(jnp.float32)
    squares = first_shard * (jnp.sum(owned[0] * owned[0]) + jnp.sum(owned[5] * owned[5]))
    for position in (1, 2, 3, 4, 6, 7, 8):
        squares = squares + jnp.sum(owned[position] * owned[position])
    global_norm = jnp.sqrt(lax.psum(squares, ("dp", "shard")))
    factor = jnp.minimum(1.0, CLIP / global_norm)
    rate_now = rate * jnp.minimum(1.0, (step.astype(jnp.float32) + 1.0) / WARMUP)
    masters = (gain_first, w_query, w_key, w_value, w_output, gain_second, w_gate, w_up, w_down)
    moments = (
        moment_first,
        moment_query,
        moment_key,
        moment_value,
        moment_output,
        moment_second,
        moment_gate,
        moment_up,
        moment_down,
    )
    momenta = [0.5 * moment + 0.5 * (factor * gradient) for moment, gradient in zip(moments, owned)]
    updated = [master - rate_now * momentum for master, momentum in zip(masters, momenta)]
    return (
        output,
        input_grad,
        global_norm,
        momenta[0],
        momenta[1],
        momenta[2],
        momenta[3],
        momenta[4],
        momenta[5],
        momenta[6],
        momenta[7],
        momenta[8],
        updated[0],
        updated[1],
        updated[2],
        updated[3],
        updated[4],
        updated[5],
        updated[6],
        updated[7],
        updated[8],
    )


def solution(mesh):
    in_specs = (
        P("dp", None),
        P("dp", None),
        P("dp", None),
        P("dp"),
        P("dp", "shard"),
        P("dp", "shard"),
        P("dp", "shard"),
        P("shard", "dp"),
        P("dp"),
        P("dp", "shard"),
        P("dp", "shard"),
        P("shard", "dp"),
        P("dp"),
        P("dp", "shard"),
        P("dp", "shard"),
        P("dp", "shard"),
        P("shard", "dp"),
        P("dp"),
        P("dp", "shard"),
        P("dp", "shard"),
        P("shard", "dp"),
        P(),
        P(),
    )
    out_specs = (
        P("dp", None),
        P("dp", None),
        P(),
        P("dp"),
        P("dp", "shard"),
        P("dp", "shard"),
        P("dp", "shard"),
        P("shard", "dp"),
        P("dp"),
        P("dp", "shard"),
        P("dp", "shard"),
        P("shard", "dp"),
        P("dp"),
        P("dp", "shard"),
        P("dp", "shard"),
        P("dp", "shard"),
        P("shard", "dp"),
        P("dp"),
        P("dp", "shard"),
        P("dp", "shard"),
        P("shard", "dp"),
    )
    return jax.shard_map(
        on_device, mesh=mesh, in_specs=in_specs, out_specs=out_specs, check_vma=False
    )
```

profile of v0, /device:TPU:0, one launch (start us, length us, event | category | flops | bytes accessed | tf_op | source)
XLA Modules:
  0.0 1819.1 jit_solution(10321602777745166804)
XLA Ops:
  11.8 22.4 %all-gather = bf16[8,1,256]{2,1,0:T(2,128)(2,1)S(1)} all-gather(bf16[1,1,256]{2,1,0:T(2,128)(2,1)S(1)} %reshape.331), channel_id=1, replica_groups=mesh['dp'=8,'shard'=4] {'dp'}, dimensions={0}, use_global_device_ids=true | all-gather | bytes 4608 | tf_op jit(solution)/shard_map/all_gather | solution.py:157
  38.9 32.9 %all_gather.28 = bf16[2048,128]{1,0:T(8,128)(2,1)S(1)} all-gather(bf16[256,128]{1,0:T(8,128)(2,1)S(1)} %convert_element_type.243), channel_id=1, replica_groups=mesh['dp'=8,'shard'=4] {'dp'}, dimensions={0}, use_global_device_ids=true | all-gather | bytes 589824 | tf_op jit(solution)/shard_map/all_gather | solution.py:160
  72.8 31.7 %all_gather.29 = bf16[2048,128]{1,0:T(8,128)(2,1)S(1)} all-gather(bf16[256,128]{1,0:T(8,128)(2,1)S(1)} %convert_element_type.245), channel_id=1, replica_groups=mesh['dp'=8,'shard'=4] {'dp'}, dimensions={0}, use_global_device_ids=true | all-gather | bytes 589824 | tf_op jit(solution)/shard_map/all_gather | solution.py:159
  116.8 30.4 %while.28 = (s32[]{:T(128)}, bf16[2,1024,4,64]{1,3,2,0:T(8,128)(2,1)}, f32[2,4,1024,1]{2,1,3,0:T(4,128)}, f32[2,4,1024,1]{2,1,3,0:T(4,128)}, bf16[2,1024,64]{1,2...) while((s32[]{:T(128)}, ...), condition=%wide.region_4.5_spmd, body=%wide.region_1.4_spmd.sunk | while | flops 1125376000 | bytes 64387236 | solution.py:197
  160.8 16.6 all-gather.1
  177.3 59.9 %all-reduce.8.cloned.1.call-done = bf16[1024,2048]{1,0:T(8,128)(2,1)} async-done(((bf16[1024,2048]{1,0:T(8,128)(2,1)}), bf16[1024,2048]{1,0:T(8,128)(2,1)}) %all-reduce.8.cloned.1.call-update) | async-done | bytes 4194320 | tf_op jit(solution)/shard_map/psum | solution.py:201
  247.8 117.3 %all-gather.12.cloned.1.call-done = bf16[2048,2048]{1,0:T(8,128)(2,1)} async-done(((bf16[256,2048]{1,0:T(8,128)(2,1)}), bf16[2048,2048]{1,0:T(8,128)(2,1)}) %all-gather.12.cloned.1.call-update) | async-done | bytes 8388624 | tf_op jit(solution)/shard_map/all_gather | solution.py:163
  365.1 14.5 fusion.112
  379.6 111.4 %all-gather.14.cloned.1.call-done = bf16[2048,2048]{1,0:T(8,128)(2,1)} async-done(((bf16[256,2048]{1,0:T(8,128)(2,1)}), bf16[2048,2048]{1,0:T(8,128)(2,1)}) %all-gather.14.cloned.1.call-update) | async-done | bytes 8388624 | tf_op jit(solution)/shard_map/all_gather | solution.py:164
  491.0 14.5 fusion.113
  505.5 111.8 %all-gather.16.cloned.1.call-done = bf16[2048,2048]{1,0:T(8,128)(2,1)} async-done(((bf16[2048,256]{1,0:T(8,128)(2,1)}), bf16[2048,2048]{1,0:T(8,128)(2,1)}) %all-gather.16.cloned.1.call-update) | async-done | bytes 8388624 | tf_op jit(solution)/shard_map/all_gather | solution.py:165
  617.3 22.1 %multiply_convert_fusion = (bf16[1024,2048]{1,0:T(8,128)(2,1)}, bf16[1024,2048]{1,0:T(8,128)(2,1)}, bf16[1024,2048]{1,0:T(8,128)(2,1)}) fusion(f32[1024,2048]{1,0:T(8,128)} %fusion.112, f32[1024,2048]{1,0:T(8,128)} %fusion.113, bf16[1024,2048]{1,0:T(8,128)(2,1)} %param.29, bf16[2048,2048]{1,0:T(8,128)(2,1)} %all-gather.16.cloned.1.call-done), kind=kOutput, calls=%fused_computation.96 | convolution fusion | flops 8623489024 | bytes 41943040 | tf_op jit(solution)/shard_map/td,fd->tf/dot_general | solution.py:221
  639.4 14.7 fusion.114
  654.1 12.2 add_convert_fusion.1
  666.4 83.8 %all-reduce.10.cloned.1.call-done = bf16[1024,2048]{1,0:T(8,128)(2,1)} async-done(((bf16[1024,2048]{1,0:T(8,128)(2,1)}), bf16[1024,2048]{1,0:T(8,128)(2,1)}) %all-reduce.10.cloned.1.call-update) | async-done | bytes 4194320 | tf_op jit(solution)/shard_map/psum | solution.py:235
  767.5 79.0 %while.29 = (s32[]{:T(128)}, f32[2,1024,4,64]{1,3,2,0:T(8,128)}, f32[2,1024,64]{1,2,0:T(8,128)}, bf16[2,1024,64]{1,2,0:T(8,128)(2,1)}, bf16[2,1024,64]{1,2,0:T(8...) while((s32[]{:T(128)}, f32[2,1024,4,64]{1,3,2,0:T(8,128)}, ...), condition=%wide.region_12.13_spmd, body=%wide.region_10.12_spmd.sunk | while | flops 2727669760 | bytes 159401328 | solution.py:246
  778.4 11.7 fusion.190
  817.8 11.7 fusion.190
  852.1 13.9 convolution_convert_fusion.3
  890.8 14.0 convolution_convert_fusion.2
  905.3 14.1 convolution_convert_fusion.1
  919.4 14.1 convolution_convert_fusion
  937.6 41.8 %reduce-scatter.12.cloned.1.call-done = bf16[256,128]{1,0:T(8,128)(2,1)} async-done(((bf16[2048,128]{1,0:T(8,128)(2,1)}), bf16[256,128]{1,0:T(8,128)(2,1)}) %reduce-scatter.12.cloned.1.call-update) | async-done | bytes 65552 | tf_op jit(solution)/shard_map/reduce_scatter | solution.py:294
  980.9 153.2 %all-reduce.12.cloned.1.call-done = (bf16[1024,2048]{1,0:T(8,128)(2,1)}, bf16[1024,2048]{1,0:T(8,128)(2,1)}) async-done(((bf16[1024,2048]{1,0:T(8,128)(2,1)}, bf16[1024,2048]{1,0:T(8,128)(2,1)}), (bf16[1024,2048]{1,0:T(8,128)(2,1)}, bf16[1024,2048]{1,0:T(8,128)(2,1)})) %all-reduce.12.cloned.1.call-update) | async-done | bytes 8388624 | tf_op jit(solution)/shard_map/psum | solution.py:212
  1139.8 22.3 %all-reduce.2 = (bf16[2048]{0:T(1024)(128)(2,1)S(1)}, bf16[2048]{0:T(1024)(128)(2,1)S(1)}) all-reduce(bf16[2048]{0:T(1024)(128)(2,1)S(1)} %get-tuple-element.132, bf16[2048]{0:T(1024)(128)(2,1)S(1)} %copy-done.43), channel_id=2, replica_groups=mesh['dp'=8,'shard'=4] {'dp'}, use_global_device_ids=true, to_apply=%region_16.17.clone | all-reduce | flops 4096 | bytes 16384
  1164.1 41.8 %reduce-scatter.8.cloned.1.call-done = bf16[256,512]{1,0:T(8,128)(2,1)} async-done(((bf16[2048,512]{1,0:T(8,128)(2,1)}), bf16[256,512]{1,0:T(8,128)(2,1)}) %reduce-scatter.8.cloned.1.call-update) | async-done | bytes 262160 | tf_op jit(solution)/shard_map/reduce_scatter | solution.py:288
  1209.5 67.7 %reduce-scatter.14.cloned.1.call-done = bf16[512,256]{1,0:T(8,128)(2,1)} async-done(((bf16[512,2048]{1,0:T(8,128)(2,1)}), bf16[512,256]{1,0:T(8,128)(2,1)}) %reduce-scatter.14.cloned.1.call-update) | async-done | bytes 262160 | tf_op jit(solution)/shard_map/reduce_scatter | solution.py:297
  1280.1 148.8 %reduce-scatter.16.cloned.1.call-done = bf16[256,2048]{1,0:T(8,128)(2,1)} async-done(((bf16[2048,2048]{1,0:T(8,128)(2,1)}), bf16[256,2048]{1,0:T(8,128)(2,1)}) %reduce-scatter.16.cloned.1.call-update) | async-done | bytes 1048592 | tf_op jit(solution)/shard_map/reduce_scatter | solution.py:303
  1431.9 148.9 %reduce-scatter.18.cloned.1.call-done = bf16[256,2048]{1,0:T(8,128)(2,1)} async-done(((bf16[2048,2048]{1,0:T(8,128)(2,1)}), bf16[256,2048]{1,0:T(8,128)(2,1)}) %reduce-scatter.18.cloned.1.call-update) | async-done | bytes 1048592 | tf_op jit(solution)/shard_map/reduce_scatter | solution.py:306
  1583.9 148.9 %reduce-scatter.20.cloned.1.call-done = bf16[2048,256]{1,0:T(8,128)(2,1)} async-done(((bf16[2048,2048]{1,0:T(8,128)(2,1)}), bf16[2048,256]{1,0:T(8,128)(2,1)}) %reduce-scatter.20.cloned.1.call-update) | async-done | bytes 1048592 | tf_op jit(solution)/shard_map/reduce_scatter | solution.py:309
  1735.9 14.7 fusion.60
  1750.7 39.0 %psum.39 = f32[]{:T(128)} all-reduce(f32[]{:T(128)S(6)} %add.221), channel_id=1, replica_groups=mesh['dp'=8,'shard'=4] {'dp','shard'}, use_global_device_ids=true, to_apply=%region_35.36 | all-reduce | flops 1 | bytes 8 | tf_op jit(solution)/shard_map/psum | solution.py:317
  (261 shorter events, 221.2 us)
Async XLA Ops:
  7.2 103.3 %all-gather.8.cloned.1.call-start = ((), (), s32[]{:S(2)}) async-start(), calls=%async_computation.7 | async-start | bytes 2359296 | tf_op jit(solution)/shard_map/all_gather | solution.py:158
  9.0 138.2 %all-gather.10.cloned.1.call-start = ((), (), s32[]{:S(2)}) async-start(), calls=%async_computation.8 | async-start | bytes 2359296 | tf_op jit(solution)/shard_map/all_gather | solution.py:161
  10.9 226.4 %all-reduce.8.cloned.1.call-start = ((), (), s32[]{:S(2)}) async-start(), calls=%async_computation.9 | async-start | bytes 8388608 | tf_op jit(solution)/shard_map/psum | solution.py:201
  11.0 93.5 %copy-start = (bf16[1024,2048]{1,0:T(8,128)(2,1)S(1)}, bf16[1024,2048]{1,0:T(8,128)(2,1)}, u32[]{:S(2)}) copy-start(bf16[1024,2048]{1,0:T(8,128)(2,1)} %param.27) | copy-start | bytes 12582916
  34.3 72.8 %copy-start.38 = (f32[8,1,256]{2,1,0:T(1,128)}, f32[8,1,256]{2,1,0:T(1,128)S(1)}, u32[]{:S(2)}) copy-start(f32[8,1,256]{2,1,0:T(1,128)S(1)} %convert_element_type.295) | copy-start | bytes 24580
  38.0 71.1 %copy-start.40 = (f32[1024]{0:T(1024)}, f32[1024]{0:T(1024)S(1)}, u32[]{:S(2)}) copy-start(f32[1024]{0:T(1024)S(1)} %get-tuple-element.218) | copy-start | bytes 12292
  71.7 37.3 %copy-start.15 = (bf16[2048,128]{1,0:T(8,128)(2,1)}, bf16[2048,128]{1,0:T(8,128)(2,1)S(1)}, u32[]{:S(2)}) copy-start(bf16[2048,128]{1,0:T(8,128)(2,1)S(1)} %all_gather.28) | copy-start | bytes 1572868
  154.0 211.2 %all-gather.12.cloned.1.call-start = ((), (), s32[]{:S(2)}) async-start(), calls=%async_computation.10 | async-start | bytes 9437184 | tf_op jit(solution)/shard_map/all_gather | solution.py:163
  155.2 335.8 %all-gather.14.cloned.1.call-start = ((), (), s32[]{:S(2)}) async-start(), calls=%async_computation.11 | async-start | bytes 9437184 | tf_op jit(solution)/shard_map/all_gather | solution.py:164
  157.9 459.3 %all-gather.16.cloned.1.call-start = ((), (), s32[]{:S(2)}) async-start(), calls=%async_computation.12 | async-start | bytes 9437184 | tf_op jit(solution)/shard_map/all_gather | solution.py:165
  160.7 589.4 %all-reduce.10.cloned.1.call-start = ((), (), s32[]{:S(2)}) async-start(), calls=%async_computation.13 | async-start | bytes 8388608 | tf_op jit(solution)/shard_map/psum | solution.py:235
  666.3 269.8 %reduce-scatter.10.cloned.1.call-start = ((), (), s32[]{:S(2)}) async-start(), calls=%async_computation.15 | async-start | bytes 589824 | tf_op jit(solution)/shard_map/reduce_scatter | solution.py:291
  767.5 79.0 %copy-start.23 = (f32[1024,32]{0,1:T(8,128)S(1)}, f32[1024,32]{0,1:T(8,128)}, u32[]{:S(2)}) copy-start(f32[1024,32]{0,1:T(8,128)} %copy-done.22) | copy-start | bytes 393220
  767.5 79.0 %copy-start.25 = (f32[1024,32]{0,1:T(8,128)S(1)}, f32[1024,32]{0,1:T(8,128)}, u32[]{:S(2)}) copy-start(f32[1024,32]{0,1:T(8,128)} %copy-done.24) | copy-start | bytes 393220
  852.0 127.5 %reduce-scatter.12.cloned.1.call-start = ((), (), s32[]{:S(2)}) async-start(), calls=%async_computation.16 | async-start | bytes 589824 | tf_op jit(solution)/shard_map/reduce_scatter | solution.py:294
  868.6 265.5 %all-reduce.12.cloned.1.call-start = ((), (), s32[]{:S(2)}) async-start(), calls=%async_computation.21 | async-start | bytes 16777216 | tf_op jit(solution)/shard_map/psum | solution.py:212
  877.3 328.6 %reduce-scatter.8.cloned.1.call-start = ((), (), s32[]{:S(2)}) async-start(), calls=%async_computation.14 | async-start | bytes 2359296 | tf_op jit(solution)/shard_map/reduce_scatter | solution.py:288
  883.6 393.6 %reduce-scatter.14.cloned.1.call-start = ((), (), s32[]{:S(2)}) async-start(), calls=%async_computation.17 | async-start | bytes 2359296 | tf_op jit(solution)/shard_map/reduce_scatter | solution.py:297
  890.7 538.2 %reduce-scatter.16.cloned.1.call-start = ((), (), s32[]{:S(2)}) async-start(), calls=%async_computation.18 | async-start | bytes 9437184 | tf_op jit(solution)/shard_map/reduce_scatter | solution.py:303
  904.8 676.1 %reduce-scatter.18.cloned.1.call-start = ((), (), s32[]{:S(2)}) async-start(), calls=%async_computation.19 | async-start | bytes 9437184 | tf_op jit(solution)/shard_map/reduce_scatter | solution.py:306
  919.4 813.5 %reduce-scatter.20.cloned.1.call-start = ((), (), s32[]{:S(2)}) async-start(), calls=%async_computation.20 | async-start | bytes 9437184 | tf_op jit(solution)/shard_map/reduce_scatter | solution.py:309
  933.5 200.6 %copy-start.39 = (f32[8,1,256]{2,1,0:T(1,128)S(1)}, f32[8,1,256]{2,1,0:T(1,128)}, u32[]{:S(2)}) copy-start(f32[8,1,256]{2,1,0:T(1,128)} %copy-done.38) | copy-start | bytes 24580
  933.5 200.6 %copy-start.41 = (f32[1024]{0:T(1024)S(1)}, f32[1024]{0:T(1024)}, u32[]{:S(2)}) copy-start(f32[1024]{0:T(1024)} %copy-done.40) | copy-start | bytes 12292
  933.5 206.3 %copy-start.43 = (bf16[2048]{0:T(1024)(128)(2,1)S(1)}, bf16[2048]{0:T(1024)(128)(2,1)}, u32[]{:S(2)}) copy-start(bf16[2048]{0:T(1024)(128)(2,1)} %get-tuple-element.130) | copy-start | bytes 12292
  933.5 802.4 %copy-start.42 = (f32[1024]{0:T(1024)S(1)}, f32[1024]{0:T(1024)}, u32[]{:S(2)}) copy-start(f32[1024]{0:T(1024)} %get-tuple-element.217) | copy-start | bytes 12292
  1162.1 573.8 %copy-start.46 = (bf16[2048]{0:T(1024)(128)(2,1)}, bf16[2048]{0:T(1024)(128)(2,1)S(1)}, u32[]{:S(2)}) copy-start(bf16[2048]{0:T(1024)(128)(2,1)S(1)} %get-tuple-element.173) | copy-start | bytes 12292
  1162.1 573.8 %copy-start.47 = (bf16[2048]{0:T(1024)(128)(2,1)}, bf16[2048]{0:T(1024)(128)(2,1)S(1)}, u32[]{:S(2)}) copy-start(bf16[2048]{0:T(1024)(128)(2,1)S(1)} %get-tuple-element.172) | copy-start | bytes 12292
  1735.9 57.5 %copy-start.31 = (bf16[256,512]{1,0:T(8,128)(2,1)S(1)}, bf16[256,512]{1,0:T(8,128)(2,1)}, u32[]{:S(2)}) copy-start(bf16[256,512]{1,0:T(8,128)(2,1)} %reduce-scatter.8.cloned.1.call-done) | copy-start | bytes 786436
  1735.9 59.9 %copy-start.34 = (f32[256,128]{1,0:T(8,128)S(1)}, f32[256,128]{1,0:T(8,128)}, u32[]{:S(2)}) copy-start(f32[256,128]{1,0:T(8,128)} %param.32) | copy-start | bytes 393220
  1735.9 65.5 %copy-start.12 = (f32[256,2048]{1,0:T(8,128)S(1)}, f32[256,2048]{1,0:T(8,128)}, u32[]{:S(2)}) copy-start(f32[256,2048]{1,0:T(8,128)} %param.36) | copy-start | bytes 6291460
  1735.9 65.5 %copy-start.19 = (bf16[256,2048]{1,0:T(8,128)(2,1)S(1)}, bf16[256,2048]{1,0:T(8,128)(2,1)}, u32[]{:S(2)}) copy-start(bf16[256,2048]{1,0:T(8,128)(2,1)} %reduce-scatter.16.cloned.1.call-done) | copy-start | bytes 3145732
  1790.5 15.5 copy-start.13
  (47 other events, 296.8 us)
Sparse Core Ops, SparseCore 0:
  10.7 58.7 all-gather.7
  72.2 52.4 all-gather.9
  154.1 83.1 all-reduce.7
  240.0 125.0 all-gather.11
  367.9 123.0 all-gather.13
  493.7 123.5 all-gather.15
  666.4 83.6 all-reduce.9
  852.1 62.0 reduce-scatter.9
  918.5 60.9 reduce-scatter.11
  981.9 152.2 all-reduce.11
  1138.2 67.5 reduce-scatter.7
  1209.8 67.3 reduce-scatter.13
  1280.8 148.0 reduce-scatter.15
  1432.8 148.0 reduce-scatter.17
  1584.4 148.4 reduce-scatter.19
where the time goes:
time: 1830 us; the launch traced here: 1820 us
  waiting for transfers between devices  1240 us (68%)
  matrix products  253 us (14%)
  blocking collectives  165 us (9%)
  other arithmetic  126 us (7%)
  between operations  24.5 us (1%)
    psum x1, waiting for transfers between devices, on_device(): lax.psum(jnp.dot(activated, down_weight, preferred_element_type=jnp.float...  153 us
    reduce_scatter x1, waiting for transfers between devices, on_device(): lax.psum_scatter(grad_up_weight.astype(jnp.bfloat16), 'dp', scatter_dimen...  149 us
    reduce_scatter x1, waiting for transfers between devices, on_device(): lax.psum_scatter(grad_down_weight.astype(jnp.bfloat16), 'dp', scatter_dim...  149 us
    reduce_scatter x1, waiting for transfers between devices, on_device(): lax.psum_scatter(grad_gate_weight.astype(jnp.bfloat16), 'dp', scatter_dim...  149 us
    all_gather x1, waiting for transfers between devices, on_device(): lax.all_gather(w_gate.astype(jnp.bfloat16), 'dp', axis=0, tiled=True)  117 us
    all_gather x1, waiting for transfers between devices, on_device(): lax.all_gather(w_down.astype(jnp.bfloat16), 'dp', axis=1, tiled=True)  112 us
    all_gather x1, waiting for transfers between devices, on_device(): lax.all_gather(w_up.astype(jnp.bfloat16), 'dp', axis=0, tiled=True)  111 us
    psum x1, waiting for transfers between devices, on_device(): lax.psum(partial_two.astype(jnp.bfloat16), 'shard').astype(jnp.float32)  83.8 us
  transfers between devices with their start and end apart: 15, of which 12 were waited for; matrix products, arithmetic and copies ran while one was open for 11% of the time, Pallas kernels for 0%

commit v1 on v0

--- a/solution.py
+++ b/solution.py
@@ -12,6 +12,17 @@
 EPS = 1e-05
 THETA = 10000000.0
 NEGATIVE = -1e30
+
+
+def collect(x, axis, dim):
+    ways = lax.axis_size(axis)
+    pieces = [x]
+    for far in range(1, ways):
+        pieces.append(
+            lax.ppermute(pieces[far - 1], axis, [(d, (d - 1) % ways) for d in range(ways)])
+        )
+    line = jnp.concatenate(pieces, axis=dim)
+    return jnp.roll(line, lax.axis_index(axis) * x.shape[dim], axis=dim)
 
 
 def inverse_rms(values):
@@ -160,7 +171,7 @@
         lax.all_gather(w_value.astype(jnp.bfloat16), "dp", axis=0, tiled=True),
         lax.all_gather(w_output.astype(jnp.bfloat16), "dp", axis=1, tiled=True),
         lax.all_gather(gain_second.astype(jnp.bfloat16), "dp", axis=0, tiled=True),
-        lax.all_gather(w_gate.astype(jnp.bfloat16), "dp", axis=0, tiled=True),
+        collect(w_gate.astype(jnp.bfloat16), "dp", 0),
         lax.all_gather(w_up.astype(jnp.bfloat16), "dp", axis=0, tiled=True),
         lax.all_gather(w_down.astype(jnp.bfloat16), "dp", axis=1, tiled=True),
     )

time: 1830 us -> 1760 us (0.962)
  waiting for transfers between devices: 1240 us -> 1100 us
  blocking collectives: 165 us -> 202 us
  starting transfers between devices: 1.24 us -> 27.1 us
  local copies, waits for them, and re-layouts: 12.7 us -> 34.1 us
    ppermute x0 -> x7, waiting for transfers between devices: none -> 164 us  [collect(): lax.ppermute(pieces[far - 1], axis, [(d, (d - 1) % ways) for d in range(w...]
    all_gather x1 -> x0, waiting for transfers between devices: 117 us -> none  [on_device(): lax.all_gather(w_gate.astype(jnp.bfloat16), 'dp', axis=0, tiled=True)]
    all_gather x1, waiting for transfers between devices: 111 us -> 0.01 us  [on_device(): lax.all_gather(w_up.astype(jnp.bfloat16), 'dp', axis=0, tiled=True)]
    psum x1, waiting for transfers between devices: 59.9 us -> 0.01 us  [on_device(): lax.psum(jnp.dot(mixed, output_weight, preferred_element_type=jnp.float32...]
    all_gather x1, blocking collectives: 16.6 us -> 53.5 us  [on_device(): lax.all_gather(gain_second.astype(jnp.bfloat16), 'dp', axis=0, tiled=True)]
    ppermute x0 -> x7, starting transfers between devices: none -> 25.9 us  [collect(): lax.ppermute(pieces[far - 1], axis, [(d, (d - 1) % ways) for d in range(w...]
    unnamed x95 -> x139, local copies, waits for them, and re-layouts: 3.14 us -> 25.5 us
  transfers between devices with their start and end apart: 15 -> 21, of which waited for: 12 -> 15; matrix products, arithmetic and copies ran while one was open for 11% -> 11% of each run, Pallas kernels for 0% -> 0%
where the time goes in v1:
time: 1760 us; the launch traced here: 1750 us
  waiting for transfers between devices  1100 us (62%)
  matrix products  249 us (14%)
  blocking collectives  202 us (11%)
  other arithmetic  119 us (7%)
  local copies, waits for them, and re-layouts  34.1 us (2%)
  starting transfers between devices  27.1 us (2%)
  between operations  24.6 us (1%)
    ppermute x7, waiting for transfers between devices, collect(): lax.ppermute(pieces[far - 1], axis, [(d, (d - 1) % ways) for d in range(w...  164 us
    psum x1, waiting for transfers between devices, on_device(): lax.psum(jnp.dot(activated, down_weight, preferred_element_type=jnp.float...  153 us
    reduce_scatter x1, waiting for transfers between devices, on_device(): lax.psum_scatter(grad_gate_weight.astype(jnp.bfloat16), 'dp', scatter_dim...  149 us
    reduce_scatter x1, waiting for transfers between devices, on_device(): lax.psum_scatter(grad_up_weight.astype(jnp.bfloat16), 'dp', scatter_dimen...  149 us
    reduce_scatter x1, waiting for transfers between devices, on_device(): lax.psum_scatter(grad_down_weight.astype(jnp.bfloat16), 'dp', scatter_dim...  149 us
    all_gather x1, waiting for transfers between devices, on_device(): lax.all_gather(w_down.astype(jnp.bfloat16), 'dp', axis=1, tiled=True)  98.2 us
    psum x1, waiting for transfers between devices, on_device(): lax.psum(partial_two.astype(jnp.bfloat16), 'shard').astype(jnp.float32)  83.9 us
    reduce_scatter x1, waiting for transfers between devices, on_device(): lax.psum_scatter(grad_output_weight.astype(jnp.bfloat16), 'dp', scatter_d...  67.9 us
  transfers between devices with their start and end apart: 21, of which 15 were waited for; matrix products, arithmetic and copies ran while one was open for 11% of the time, Pallas kernels for 0%

profile of v1, /device:TPU:0, one launch (start us, length us, event | category | flops | bytes accessed | tf_op | source)
XLA Modules:
  0.0 1753.0 jit_solution(3272889996596843042)
XLA Ops:
  15.5 22.3 %all-gather = bf16[8,1,256]{2,1,0:T(2,128)(2,1)S(1)} all-gather(bf16[1,1,256]{2,1,0:T(2,128)(2,1)S(1)} %reshape.331), channel_id=1, replica_groups=mesh['dp'=8,'shard'=4] {'dp'}, dimensions={0}, use_global_device_ids=true | all-gather | bytes 4608 | tf_op jit(solution)/shard_map/all_gather | solution.py:168
  38.8 33.0 %all_gather.26 = bf16[2048,128]{1,0:T(8,128)(2,1)S(1)} all-gather(bf16[256,128]{1,0:T(8,128)(2,1)S(1)} %convert_element_type.245), channel_id=1, replica_groups=mesh['dp'=8,'shard'=4] {'dp'}, dimensions={0}, use_global_device_ids=true | all-gather | bytes 589824 | tf_op jit(solution)/shard_map/all_gather | solution.py:170
  72.8 31.7 %all_gather.25 = bf16[2048,128]{1,0:T(8,128)(2,1)S(1)} all-gather(bf16[256,128]{1,0:T(8,128)(2,1)S(1)} %convert_element_type.243), channel_id=1, replica_groups=mesh['dp'=8,'shard'=4] {'dp'}, dimensions={0}, use_global_device_ids=true | all-gather | bytes 589824 | tf_op jit(solution)/shard_map/all_gather | solution.py:171
  115.4 28.4 %while.28 = (s32[]{:T(128)}, bf16[2,1024,4,64]{1,3,2,0:T(8,128)(2,1)}, f32[2,4,1024,1]{2,1,3,0:T(4,128)}, f32[2,4,1024,1]{2,1,3,0:T(4,128)}, bf16[2,1024,64]{1,2...) while((s32[]{:T(128)}, ...), condition=%wide.region_4.5_spmd, body=%wide.region_1.4_spmd.sunk | while | flops 1125376000 | bytes 64387736 | solution.py:208
  158.3 23.9 %collective-permute-done = bf16[256,2048]{1,0:T(8,128)(2,1)S(1)} collective-permute-done((bf16[256,2048]{1,0:T(8,128)(2,1)S(1)}, bf16[256,2048]{1,0:T(8,128)(2,1)S(1)}, u32[]{:S(2)}, u32[]{:S(2)}) %collective-permute-start) | collective-permute-done | bytes 1048608 | tf_op jit(solution)/shard_map/ppermute | solution.py:22
  186.7 22.8 %collective-permute-done.1 = bf16[256,2048]{1,0:T(8,128)(2,1)S(1)} collective-permute-done((bf16[256,2048]{1,0:T(8,128)(2,1)S(1)}, bf16[256,2048]{1,0:T(8,128)(2,1)S(1)}, u32[]{:S(2)}, u32[]{:S(2)}) %collective-permute-start.1) | collective-permute-done | bytes 1048608 | tf_op jit(solution)/shard_map/ppermute | solution.py:22
  214.7 22.0 %collective-permute-done.2 = bf16[256,2048]{1,0:T(8,128)(2,1)S(1)} collective-permute-done((bf16[256,2048]{1,0:T(8,128)(2,1)S(1)}, bf16[256,2048]{1,0:T(8,128)(2,1)S(1)}, u32[]{:S(2)}, u32[]{:S(2)}) %collective-permute-start.2) | collective-permute-done | bytes 1048608 | tf_op jit(solution)/shard_map/ppermute | solution.py:22
  241.8 40.4 %collective-permute-done.3 = bf16[256,2048]{1,0:T(8,128)(2,1)} collective-permute-done((bf16[256,2048]{1,0:T(8,128)(2,1)S(1)}, bf16[256,2048]{1,0:T(8,128)(2,1)}, u32[]{:S(2)}, u32[]{:S(2)}) %collective-permute-start.3) | collective-permute-done | bytes 1048608 | tf_op jit(solution)/shard_map/ppermute | solution.py:22
  287.6 53.5 %all-gather.1 = bf16[8,1,256]{2,1,0:T(2,128)(2,1)S(1)} all-gather(bf16[1,1,256]{2,1,0:T(2,128)(2,1)S(1)} %reshape.333), channel_id=1, replica_groups=mesh['dp'=8,'shard'=4] {'dp'}, dimensions={0}, use_global_device_ids=true | all-gather | bytes 4608 | tf_op jit(solution)/shard_map/all_gather | solution.py:173
  353.9 32.9 %collective-permute-done.5 = bf16[256,2048]{1,0:T(8,128)(2,1)} collective-permute-done((bf16[256,2048]{1,0:T(8,128)(2,1)}, bf16[256,2048]{1,0:T(8,128)(2,1)}, u32[]{:S(2)}, u32[]{:S(2)}) %collective-permute-start.5) | collective-permute-done | bytes 1048608 | tf_op jit(solution)/shard_map/ppermute | solution.py:22
  398.9 21.9 %collective-permute-done.6 = bf16[256,2048]{1,0:T(8,128)(2,1)S(1)} collective-permute-done((bf16[256,2048]{1,0:T(8,128)(2,1)}, bf16[256,2048]{1,0:T(8,128)(2,1)S(1)}, u32[]{:S(2)}, u32[]{:S(2)}) %collective-permute-start.6) | collective-permute-done | bytes 1048608 | tf_op jit(solution)/shard_map/ppermute | solution.py:22
  434.3 14.5 fusion.120
  448.7 98.2 %all-gather.13.cloned.1.call-done = bf16[2048,2048]{1,0:T(8,128)(2,1)} async-done(((bf16[2048,256]{1,0:T(8,128)(2,1)}), bf16[2048,2048]{1,0:T(8,128)(2,1)}) %all-gather.13.cloned.1.call-update) | async-done | bytes 8388624 | tf_op jit(solution)/shard_map/all_gather | solution.py:176
  547.0 14.7 fusion.121
  561.7 19.9 %multiply_convert_fusion.1 = (bf16[1024,2048]{1,0:T(8,128)(2,1)}, bf16[1024,2048]{1,0:T(8,128)(2,1)}, bf16[1024,2048]{1,0:T(8,128)(2,1)}) fusion(f32[1024,2048]{1,0:T(8,128)} %fusion.121, f32[1024,2048]{1,0:T(8,128)} %fusion.120, bf16[1024,2048]{1,0:T(8,128)(2,1)S(1)} %copy-done.19, bf16[4096,2048]{1,0:T(8,128)(2,1)} %constant_dynamic-update-slice_fusion, ...), kind=kOutput, calls=%fused_computation.97 | convolution fusion | flops 8623489024 | bytes 41943044 | tf_op jit(solution)/shard_map/dot_general | solution.py:219
  594.2 12.8 add_convert_fusion.1
  607.2 83.9 %all-reduce.10.cloned.1.call-done = bf16[1024,2048]{1,0:T(8,128)(2,1)} async-done(((bf16[1024,2048]{1,0:T(8,128)(2,1)}), bf16[1024,2048]{1,0:T(8,128)(2,1)}) %all-reduce.10.cloned.1.call-update) | async-done | bytes 4194320 | tf_op jit(solution)/shard_map/psum | solution.py:246
  708.1 77.4 %while.29 = (s32[]{:T(128)}, f32[2,1024,4,64]{1,3,2,0:T(8,128)}, f32[2,1024,64]{1,2,0:T(8,128)}, bf16[2,1024,64]{1,2,0:T(8,128)(2,1)}, bf16[2,1024,64]{1,2,0:T(8...) while((s32[]{:T(128)}, f32[2,1024,4,64]{1,3,2,0:T(8,128)}, ...), condition=%wide.region_12.13_spmd, body=%wide.region_10.12_spmd.sunk | while | flops 2727669760 | bytes 158352688 | solution.py:257
  791.1 14.0 convolution_convert_fusion.3
  831.8 14.2 convolution_convert_fusion.2
  846.4 14.1 convolution_convert_fusion.1
  860.5 14.1 convolution_convert_fusion
  878.8 39.7 %reduce-scatter.12.cloned.1.call-done = bf16[256,128]{1,0:T(8,128)(2,1)} async-done(((bf16[2048,128]{1,0:T(8,128)(2,1)}), bf16[256,128]{1,0:T(8,128)(2,1)}) %reduce-scatter.12.cloned.1.call-update) | async-done | bytes 65552 | tf_op jit(solution)/shard_map/reduce_scatter | solution.py:305
  919.9 153.4 %all-reduce.12.cloned.1.call-done = (bf16[1024,2048]{1,0:T(8,128)(2,1)}, bf16[1024,2048]{1,0:T(8,128)(2,1)}) async-done(((bf16[1024,2048]{1,0:T(8,128)(2,1)}, bf16[1024,2048]{1,0:T(8,128)(2,1)}), (bf16[1024,2048]{1,0:T(8,128)(2,1)}, bf16[1024,2048]{1,0:T(8,128)(2,1)})) %all-reduce.12.cloned.1.call-update) | async-done | bytes 8388624 | tf_op jit(solution)/shard_map/psum | solution.py:223
  1078.9 22.3 %all-reduce.2 = (bf16[2048]{0:T(1024)(128)(2,1)S(1)}, bf16[2048]{0:T(1024)(128)(2,1)S(1)}) all-reduce(bf16[2048]{0:T(1024)(128)(2,1)S(1)} %get-tuple-element.132, bf16[2048]{0:T(1024)(128)(2,1)S(1)} %copy-done.56), channel_id=2, replica_groups=mesh['dp'=8,'shard'=4] {'dp'}, use_global_device_ids=true, to_apply=%region_16.17.clone | all-reduce | flops 4096 | bytes 16384
  1103.2 41.8 %reduce-scatter.8.cloned.1.call-done = bf16[256,512]{1,0:T(8,128)(2,1)} async-done(((bf16[2048,512]{1,0:T(8,128)(2,1)}), bf16[256,512]{1,0:T(8,128)(2,1)}) %reduce-scatter.8.cloned.1.call-update) | async-done | bytes 262160 | tf_op jit(solution)/shard_map/reduce_scatter | solution.py:299
  1148.6 67.9 %reduce-scatter.14.cloned.1.call-done = bf16[512,256]{1,0:T(8,128)(2,1)} async-done(((bf16[512,2048]{1,0:T(8,128)(2,1)}), bf16[512,256]{1,0:T(8,128)(2,1)}) %reduce-scatter.14.cloned.1.call-update) | async-done | bytes 262160 | tf_op jit(solution)/shard_map/reduce_scatter | solution.py:308
  1218.9 149.1 %reduce-scatter.16.cloned.1.call-done = bf16[256,2048]{1,0:T(8,128)(2,1)} async-done(((bf16[2048,2048]{1,0:T(8,128)(2,1)}), bf16[256,2048]{1,0:T(8,128)(2,1)}) %reduce-scatter.16.cloned.1.call-update) | async-done | bytes 1048592 | tf_op jit(solution)/shard_map/reduce_scatter | solution.py:314
  1371.0 149.1 %reduce-scatter.18.cloned.1.call-done = bf16[256,2048]{1,0:T(8,128)(2,1)} async-done(((bf16[2048,2048]{1,0:T(8,128)(2,1)}), bf16[256,2048]{1,0:T(8,128)(2,1)}) %reduce-scatter.18.cloned.1.call-update) | async-done | bytes 1048592 | tf_op jit(solution)/shard_map/reduce_scatter | solution.py:317
  1523.1 148.9 %reduce-scatter.20.cloned.1.call-done = bf16[2048,256]{1,0:T(8,128)(2,1)} async-done(((bf16[2048,2048]{1,0:T(8,128)(2,1)}), bf16[2048,256]{1,0:T(8,128)(2,1)}) %reduce-scatter.20.cloned.1.call-update) | async-done | bytes 1048592 | tf_op jit(solution)/shard_map/reduce_scatter | solution.py:320
  1675.1 14.8 fusion.60
  1689.9 39.1 %psum.39 = f32[]{:T(128)} all-reduce(f32[]{:T(128)S(6)} %add.233), channel_id=1, replica_groups=mesh['dp'=8,'shard'=4] {'dp','shard'}, use_global_device_ids=true, to_apply=%region_35.36 | all-reduce | flops 1 | bytes 8 | tf_op jit(solution)/shard_map/psum | solution.py:328
  (313 shorter events, 296.7 us)
Async XLA Ops:
  7.2 102.5 %all-gather.7.cloned.1.call-start = ((), (), s32[]{:S(2)}) async-start(), calls=%async_computation.7 | async-start | bytes 2359296 | tf_op jit(solution)/shard_map/all_gather | solution.py:169
  9.0 134.8 %all-gather.9.cloned.1.call-start = ((), (), s32[]{:S(2)}) async-start(), calls=%async_computation.8 | async-start | bytes 2359296 | tf_op jit(solution)/shard_map/all_gather | solution.py:172
  10.9 338.0 %all-reduce.8.cloned.1.call-start = ((), (), s32[]{:S(2)}) async-start(), calls=%async_computation.9 | async-start | bytes 8388608 | tf_op jit(solution)/shard_map/psum | solution.py:212
  11.0 93.4 %copy-start = (bf16[1024,2048]{1,0:T(8,128)(2,1)S(1)}, bf16[1024,2048]{1,0:T(8,128)(2,1)}, u32[]{:S(2)}) copy-start(bf16[1024,2048]{1,0:T(8,128)(2,1)} %param.27) | copy-start | bytes 12582916
  14.8 92.2 %copy-start.53 = (f32[1024]{0:T(1024)}, f32[1024]{0:T(1024)S(1)}, u32[]{:S(2)}) copy-start(f32[1024]{0:T(1024)S(1)} %get-tuple-element.220) | copy-start | bytes 12292
  37.8 69.2 %copy-start.51 = (f32[8,1,256]{2,1,0:T(1,128)}, f32[8,1,256]{2,1,0:T(1,128)S(1)}, u32[]{:S(2)}) copy-start(f32[8,1,256]{2,1,0:T(1,128)S(1)} %convert_element_type.295) | copy-start | bytes 24580
  151.0 136.6 %copy-start.58 = (f32[256]{0:T(256)S(1)}, f32[256]{0:T(256)}, u32[]{:S(2)}) copy-start(f32[256]{0:T(256)} %param.35) | copy-start | bytes 3076
  151.0 283.3 %all-gather.11.cloned.1.call-start = ((), (), s32[]{:S(2)}) async-start(), calls=%async_computation.10 | async-start | bytes 9437184 | tf_op jit(solution)/shard_map/all_gather | solution.py:175
  153.8 393.2 %all-gather.13.cloned.1.call-start = ((), (), s32[]{:S(2)}) async-start(), calls=%async_computation.11 | async-start | bytes 9437184 | tf_op jit(solution)/shard_map/all_gather | solution.py:176
  155.0 536.1 %all-reduce.10.cloned.1.call-start = ((), (), s32[]{:S(2)}) async-start(), calls=%async_computation.12 | async-start | bytes 8388608 | tf_op jit(solution)/shard_map/psum | solution.py:246
  157.8 124.4 %copy-start.22 = (bf16[256,2048]{1,0:T(8,128)(2,1)}, bf16[256,2048]{1,0:T(8,128)(2,1)S(1)}, u32[]{:S(2)}) copy-start(bf16[256,2048]{1,0:T(8,128)(2,1)S(1)} %get-tuple-element.177) | copy-start | bytes 3145732
  157.8 24.5 %collective-permute-start = (bf16[256,2048]{1,0:T(8,128)(2,1)S(1)}, bf16[256,2048]{1,0:T(8,128)(2,1)S(1)}, u32[]{:S(2)}, u32[]{:S(2)}) collective-permute-start(bf16[256,2048]{1,0:T(8,128)(2,1)S(1)} %get-tuple-element.177), channel_id=1, source_target_pairs={{0,28},{4,0},{8,4},{12,8},{16,12},{20,16},{24,20},{28,24},{1,29},{... | collective-permute-start | bytes 3145736 | tf_op jit(solution)/shard_map/ppermute | solution.py:22
  182.3 27.2 %collective-permute-start.1 = (bf16[256,2048]{1,0:T(8,128)(2,1)S(1)}, bf16[256,2048]{1,0:T(8,128)(2,1)S(1)}, u32[]{:S(2)}, u32[]{:S(2)}) collective-permute-start(bf16[256,2048]{1,0:T(8,128)(2,1)S(1)} %collective-permute-done), channel_id=1, source_target_pairs={{0,28},{4,0},{8,4},{12,8},{16,12},{20,16},{24,20},{28,24},{1,29},{... | collective-permute-start | bytes 3145736 | tf_op jit(solution)/shard_map/ppermute | solution.py:22
  209.5 27.1 %collective-permute-start.2 = (bf16[256,2048]{1,0:T(8,128)(2,1)S(1)}, bf16[256,2048]{1,0:T(8,128)(2,1)S(1)}, u32[]{:S(2)}, u32[]{:S(2)}) collective-permute-start(bf16[256,2048]{1,0:T(8,128)(2,1)S(1)} %collective-permute-done.1), channel_id=1, source_target_pairs={{0,28},{4,0},{8,4},{12,8},{16,12},{20,16},{24,20},{28,24},{1,29},{... | collective-permute-start | bytes 3145736 | tf_op jit(solution)/shard_map/ppermute | solution.py:22
  236.6 45.6 %collective-permute-start.3 = (bf16[256,2048]{1,0:T(8,128)(2,1)S(1)}, bf16[256,2048]{1,0:T(8,128)(2,1)}, u32[]{:S(2)}, u32[]{:S(2)}) collective-permute-start(bf16[256,2048]{1,0:T(8,128)(2,1)S(1)} %collective-permute-done.2), channel_id=1, source_target_pairs={{0,28},{4,0},{8,4},{12,8},{16,12},{20,16},{24,20},{28,24},{1,29},{... | collective-permute-start | bytes 3145736 | tf_op jit(solution)/shard_map/ppermute | solution.py:22
  282.2 62.0 %collective-permute-start.4 = (bf16[256,2048]{1,0:T(8,128)(2,1)}, bf16[256,2048]{1,0:T(8,128)(2,1)}, u32[]{:S(2)}, u32[]{:S(2)}) collective-permute-start(bf16[256,2048]{1,0:T(8,128)(2,1)} %collective-permute-done.3), channel_id=1, source_target_pairs={{0,28},{4,0},{8,4},{12,8},{16,12},{20,16},{24,20},{28,24},{1,29},{... | collective-permute-start | bytes 3145736 | tf_op jit(solution)/shard_map/ppermute | solution.py:22
  344.2 42.6 %collective-permute-start.5 = (bf16[256,2048]{1,0:T(8,128)(2,1)}, bf16[256,2048]{1,0:T(8,128)(2,1)}, u32[]{:S(2)}, u32[]{:S(2)}) collective-permute-start(bf16[256,2048]{1,0:T(8,128)(2,1)} %collective-permute-done.4), channel_id=1, source_target_pairs={{0,28},{4,0},{8,4},{12,8},{16,12},{20,16},{24,20},{28,24},{1,29},{... | collective-permute-start | bytes 3145736 | tf_op jit(solution)/shard_map/ppermute | solution.py:22
  386.7 34.0 %collective-permute-start.6 = (bf16[256,2048]{1,0:T(8,128)(2,1)}, bf16[256,2048]{1,0:T(8,128)(2,1)S(1)}, u32[]{:S(2)}, u32[]{:S(2)}) collective-permute-start(bf16[256,2048]{1,0:T(8,128)(2,1)} %collective-permute-done.5), channel_id=1, source_target_pairs={{0,28},{4,0},{8,4},{12,8},{16,12},{20,16},{24,20},{28,24},{1,29},{... | collective-permute-start | bytes 3145736 | tf_op jit(solution)/shard_map/ppermute | solution.py:22
  607.1 270.2 %reduce-scatter.10.cloned.1.call-start = ((), (), s32[]{:S(2)}) async-start(), calls=%async_computation.14 | async-start | bytes 589824 | tf_op jit(solution)/shard_map/reduce_scatter | solution.py:302
  708.1 77.4 %copy-start.25 = (f32[1024,32]{0,1:T(8,128)S(1)}, f32[1024,32]{0,1:T(8,128)}, u32[]{:S(2)}) copy-start(f32[1024,32]{0,1:T(8,128)} %copy-done.24) | copy-start | bytes 393220
  708.1 77.4 %copy-start.27 = (f32[1024,32]{0,1:T(8,128)S(1)}, f32[1024,32]{0,1:T(8,128)}, u32[]{:S(2)}) copy-start(f32[1024,32]{0,1:T(8,128)} %copy-done.26) | copy-start | bytes 393220
  791.0 127.5 %reduce-scatter.12.cloned.1.call-start = ((), (), s32[]{:S(2)}) async-start(), calls=%async_computation.15 | async-start | bytes 589824 | tf_op jit(solution)/shard_map/reduce_scatter | solution.py:305
  808.7 264.6 %all-reduce.12.cloned.1.call-start = ((), (), s32[]{:S(2)}) async-start(), calls=%async_computation.20 | async-start | bytes 16777216 | tf_op jit(solution)/shard_map/psum | solution.py:223
  818.3 326.7 %reduce-scatter.8.cloned.1.call-start = ((), (), s32[]{:S(2)}) async-start(), calls=%async_computation.13 | async-start | bytes 2359296 | tf_op jit(solution)/shard_map/reduce_scatter | solution.py:299
  824.6 391.9 %reduce-scatter.14.cloned.1.call-start = ((), (), s32[]{:S(2)}) async-start(), calls=%async_computation.16 | async-start | bytes 2359296 | tf_op jit(solution)/shard_map/reduce_scatter | solution.py:308
  831.7 536.3 %reduce-scatter.16.cloned.1.call-start = ((), (), s32[]{:S(2)}) async-start(), calls=%async_computation.17 | async-start | bytes 9437184 | tf_op jit(solution)/shard_map/reduce_scatter | solution.py:314
  845.9 674.2 %reduce-scatter.18.cloned.1.call-start = ((), (), s32[]{:S(2)}) async-start(), calls=%async_computation.18 | async-start | bytes 9437184 | tf_op jit(solution)/shard_map/reduce_scatter | solution.py:317
  860.5 811.6 %reduce-scatter.20.cloned.1.call-start = ((), (), s32[]{:S(2)}) async-start(), calls=%async_computation.19 | async-start | bytes 9437184 | tf_op jit(solution)/shard_map/reduce_scatter | solution.py:320
  874.7 198.6 %copy-start.52 = (f32[8,1,256]{2,1,0:T(1,128)S(1)}, f32[8,1,256]{2,1,0:T(1,128)}, u32[]{:S(2)}) copy-start(f32[8,1,256]{2,1,0:T(1,128)} %copy-done.51) | copy-start | bytes 24580
  874.7 198.6 %copy-start.54 = (f32[1024]{0:T(1024)S(1)}, f32[1024]{0:T(1024)}, u32[]{:S(2)}) copy-start(f32[1024]{0:T(1024)} %copy-done.53) | copy-start | bytes 12292
  874.7 204.2 %copy-start.56 = (bf16[2048]{0:T(1024)(128)(2,1)S(1)}, bf16[2048]{0:T(1024)(128)(2,1)}, u32[]{:S(2)}) copy-start(bf16[2048]{0:T(1024)(128)(2,1)} %get-tuple-element.130) | copy-start | bytes 12292
  874.7 800.4 %copy-start.55 = (f32[1024]{0:T(1024)S(1)}, f32[1024]{0:T(1024)}, u32[]{:S(2)}) copy-start(f32[1024]{0:T(1024)} %get-tuple-element.219) | copy-start | bytes 12292
  (66 other events, 782.2 us)
Sparse Core Ops, SparseCore 0:
  10.7 58.5 all-gather.6
  71.9 52.8 all-gather.8
  151.1 82.6 all-reduce.7
  236.6 181.0 all-gather.10
  420.3 126.5 all-gather.12
  607.2 83.7 all-reduce.9
  791.1 62.0 reduce-scatter.9
  857.5 60.9 reduce-scatter.11
  921.0 152.2 all-reduce.11
  1077.3 67.6 reduce-scatter.7
  1149.1 67.3 reduce-scatter.13
  1220.0 147.9 reduce-scatter.15
  1372.1 148.0 reduce-scatter.17
  1523.6 148.4 reduce-scatter.19
